TPU v7x, 32 devices: a whole 2x2x4 slice. The times are simulated.
32 devices in a mesh: row: 8 (over y, x, core), col: 4 (over z).
Axes of the slice: x: 2, y: 2, z: 4, core: 2. Of those that a mesh axis runs over, the one named last changes fastest.
Arguments:
- positions: float32 [3, 32768], P(None, ('row', 'col')), may hold values from 0 to 1
- segments: float32 [3, 32768], P(None, ('row', 'col')), may hold values from -1.2 to 1.2
- radius: float32 [32768], P(('row', 'col')), may hold values from 0.05 to 0.2
- currents: float32 [2, 32768], P(None, ('row', 'col')), may hold values from -6 to 6
- resist: float32 [32768], P(('row', 'col')), may hold values from 0.3 to 3
- slot_of: int32 [32768], P(('row', 'col')), may hold values from 0 to 1023, as said below
- pair_list: int32 [1024, 2], P(('row', 'col')), may hold values from 0 to 63, as said below
- near_flag: int32 [1024], P(('row', 'col')), may hold values from 0 to 2, as said below
Outputs:
- voltage: float32 [2, 32768], P(None, ('row', 'col'))
Inputs may be any that keep to these rules, and one draw needn't show every extreme that they name: `slot_of`: the elements of shard d hold the values 0 to 1023 once each; a value s puts the element in cluster d * 2 + s // 512. `pair_list`: shard d = r * 4 + c lists 32 slots; each live slot holds a pair (I, J) with I <= J, I in clusters r * 2 * 4 to (r + 1) * 2 * 4 - 1 and (J // 2) % 4 = c; a pair stands in one live slot at most, over all shards. Empty slots hold I = r * 2 * 4 and J = c * 2. `near_flag`: 0 marks an empty slot.
All inputs are finite; a program needn't handle non-finite values.
Results may differ from a plain program's by a relative error of at most 0.0003.
Values sent between devices are 32-bit elements; how exact they have to be, the bound alone decides.
A program may use at most 64 MiB of HBM per device.

v0:
```python
import functools
import math

import jax
import jax.numpy as jnp
from jax import lax
from jax.experimental import pallas as pl
from jax.experimental.pallas import tpu as pltpu
from jax.sharding import PartitionSpec as P

CS = 512
F32 = jnp.float32
BF16 = jnp.bfloat16
MESH = pl.DeviceIdType.MESH
gauss_step = 0.5 / math.sqrt(3.0)
kernel_gain = 0.25
VMEM = pl.BlockSpec(memory_space=pltpu.VMEM)
TALL = 256
WIDE = 512
FAR = 2


def split_three(value):
    high = value.astype(BF16).astype(F32)
    rest = value - high
    middle = rest.astype(BF16).astype(F32)
    return high, middle, rest - middle


def dot_nn(left, right):
    return lax.dot_general(left, right, (((1,), (0,)), ((), ())), preferred_element_type=F32)


def dot_nt(left, right):
    return lax.dot_general(left, right, (((1,), (1,)), ((), ())), preferred_element_type=F32)


def one_hot_rows(slots, start, count):
    rows = lax.broadcasted_iota(jnp.int32, (count, slots.shape[1]), 0) + start
    return jnp.where(rows == slots, 1.0, 0.0).astype(BF16)


def order_into(pos, seg, rad, cur, slot, pair, flag, main, extra, stack):
    clusters = main.shape[0]
    slots = slot[...]
    stack[...] = jnp.zeros_like(stack)
    for source, row in ((pos, 0), (seg, 3), (rad, 6), (cur, 7)):
        count = source.shape[0]
        for part, piece in enumerate(split_three(source[...])):
            stack[part * 16 + row : part * 16 + row + count, :] = piece
    parts = stack[...].astype(BF16)
    for cluster in range(clusters):
        sums = dot_nt(parts, one_hot_rows(slots, cluster * CS, CS))
        ordered = sums[0:16] + sums[16:32] + sums[32:48]
        main[cluster] = ordered[0:8]
        extra[cluster : cluster + 1, :] = ordered[8:9]
    listed = pair.shape[1]
    extra[clusters : clusters + 2, :] = jnp.zeros((2, CS), F32)
    extra[clusters : clusters + 1, 0:listed] = pair[0:1, :].astype(F32)
    extra[clusters : clusters + 1, 128 : 128 + listed] = pair[1:2, :].astype(F32)
    extra[clusters : clusters + 1, 256 : 256 + listed] = flag[...].astype(F32)


def pair_kernel(main, extra, total, feat_first, feat_second, weight_first, weight_second):
    devices, clusters = main.shape[0], main.shape[1]
    me = lax.axis_index("row") * lax.axis_size("col") + lax.axis_index("col")
    total[...] = jnp.zeros_like(total)
    for feat, ones in ((feat_first, 21), (feat_second, 18)):
        feat[...] = jnp.zeros_like(feat)
        for unit in range(FAR):
            for sign in range(2):
                feat[unit, sign, ones : ones + 3, :] = jnp.ones((3, CS), F32)
    weight_first[...] = jnp.zeros_like(weight_first)
    weight_second[...] = jnp.zeros_like(weight_second)

    lists = extra[:, clusters, :]
    first_ids, second_ids, flags = lists[:, 0:128], lists[:, 128:256], lists[:, 256:384]
    code = (first_ids * 1024.0 + second_ids) * 4.0 + flags
    is_near = jnp.where(flags > 1.5, 1.0, 0.0)
    is_far = jnp.where(jnp.abs(flags - 1.0) < 0.5, 1.0, 0.0)
    before_lane = jnp.where(
        lax.broadcasted_iota(jnp.int32, (128, 128), 0) < lax.broadcasted_iota(jnp.int32, (128, 128), 1),
        1.0,
        0.0,
    ).astype(BF16)
    before_row = jnp.where(
        lax.broadcasted_iota(jnp.int32, (devices, devices), 1)
        < lax.broadcasted_iota(jnp.int32, (devices, devices), 0),
        1.0,
        0.0,
    ).astype(BF16)

    def rank_in(mask):
        in_row = dot_nn(mask.astype(BF16), before_lane)
        above = jnp.sum(dot_nn(before_row, mask.astype(BF16)), axis=1, keepdims=True)
        return in_row + above

    near_count = jnp.sum(is_near)
    live_count = near_count + jnp.sum(is_far)
    rank = jnp.where(
        is_near > 0.5,
        rank_in(is_near),
        jnp.where(is_far > 0.5, rank_in(is_far) + near_count, -1.0),
    ).astype(jnp.int32)
    def share(count):
        return (count.astype(jnp.int32) + (devices - 1 - me)) // devices

    mine_near, mine = share(near_count), share(live_count)

    def pick(turn):
        found = jnp.where(rank == turn * devices + me, code, 0.0)
        return jnp.sum(found).astype(jnp.int32)

    def load(cluster, weights):
        device, local = cluster // clusters, cluster % clusters
        block = main[device, local]
        imag = extra[device, pl.ds(local, 1), :]
        for axis in range(3):
            vector = block[3 + axis : 4 + axis]
            for part, current in enumerate((block[7:8], imag)):
                product = vector * current
                high = product.astype(BF16).astype(F32)
                row = 2 * axis + part
                weights[row : row + 1, :] = high
                weights[8 + row : 9 + row, :] = product - high
        return block

    def write(feat, points, radii, gain, order, norm_row):
        norm = jnp.sum(points * points, axis=0, keepdims=True) + radii * radii
        parts = split_three(gain * points)
        for slot, part in enumerate(order):
            feat[3 * slot : 3 * slot + 3, :] = parts[part]
        for row, piece in enumerate(split_three(norm)):
            feat[norm_row + row : norm_row + row + 1, :] = piece

    def contract(sums, block, scale):
        both = sums[0:8] + sums[8:16]
        result = 0.0
        for axis in range(3):
            result = result + both[2 * axis : 2 * axis + 2] * block[3 + axis : 4 + axis]
        return result * scale

    def apply(codes_and_scales, signs):
        units = []
        for unit, (now, scale) in enumerate(codes_and_scales):
            first, second = now // 4096, now // 4 % 1024
            block_first = load(first, weight_first.at[unit])
            block_second = load(second, weight_second.at[unit])
            for sign in range(signs):
                step = gauss_step if sign else -gauss_step
                for block, feat, gain, order, norm_row in (
                    (block_first, feat_first, 1.0, (0, 0, 1, 1, 0, 2), 18),
                    (block_second, feat_second, -2.0, (0, 1, 0, 1, 2, 0), 21),
                ):
                    points = block[0:3] - 0.5
                    if signs > 1:
                        points = points + step * block[3:6]
                    write(feat.at[unit, sign], points, block[6:7], gain, order, norm_row)
            units.append((unit, first, second, block_first, block_second, scale))
        sides = []
        for unit, *_ in units:
            left = [feat_first[unit, sign].T.astype(BF16) for sign in range(signs)]
            right = [feat_second[unit, sign].astype(BF16) for sign in range(signs)]
            from_first = weight_first[unit].astype(BF16)
            turned = weight_second[unit].T.astype(BF16)
            sides.append((left, right, from_first, turned))
        mirrors = [[0.0 for _ in range(0, CS, WIDE)] for _ in units]
        directs = [[] for _ in units]
        for start in range(0, CS, TALL):
            sums = [0.0 for _ in units]
            for index, across in enumerate(range(0, CS, WIDE)):
                for unit, (left, right, from_first, turned) in enumerate(sides):
                    inverse = 0.0
                    for one in left:
                        for other in right:
                            inverse = inverse + lax.rsqrt(
                                dot_nn(one[start : start + TALL], other[:, across : across + WIDE])
                            )
                    high = inverse.astype(BF16)
                    low = (inverse - high.astype(F32)).astype(BF16)
                    near_side = turned[across : across + WIDE]
                    rows = from_first[:, start : start + TALL]
                    sums[unit] = sums[unit] + dot_nn(high, near_side) + dot_nn(low, near_side)
                    mirrors[unit][index] = (
                        mirrors[unit][index] + dot_nn(rows, high) + dot_nn(rows, low)
                    )
            for unit, _ in enumerate(units):
                directs[unit].append(sums[unit])
        terms = []
        for unit, first, second, block_first, block_second, scale in units:
            direct = jnp.concatenate(directs[unit], 0).T
            mirror = jnp.concatenate(mirrors[unit], 1)
            keep = jnp.where(first == second, 0.0, scale)
            terms.append((first, contract(direct, block_first, scale)))
            terms.append((second, contract(mirror, block_second, keep)))
        for cluster, term in terms:
            total[cluster] += term

    def visit_near(turn, now):
        apply([(now, kernel_gain * 0.25)], 2)
        return pick(turn + 1)

    def visit_far(step, codes):
        turn = mine_near + FAR * step
        apply(
            [
                (now, kernel_gain if unit == 0 else jnp.where(turn + unit < mine, kernel_gain, 0.0))
                for unit, now in enumerate(codes)
            ],
            1,
        )
        return tuple(pick(turn + FAR + unit) for unit in range(FAR))

    start = lax.fori_loop(0, mine_near, visit_near, pick(0))
    lax.fori_loop(
        0,
        (mine - mine_near + FAR - 1) // FAR,
        visit_far,
        (start,) + tuple(pick(mine_near + unit) for unit in range(1, FAR)),
    )


def pair_terms(main, extra):
    devices, clusters = main.shape[0], main.shape[1]
    return pl.pallas_call(
        pair_kernel,
        out_shape=jax.ShapeDtypeStruct((devices * clusters, 2, CS), F32),
        in_specs=[VMEM, VMEM],
        out_specs=VMEM,
        scratch_shapes=[
            pltpu.VMEM((FAR, 2, 32, CS), F32),
            pltpu.VMEM((FAR, 2, 32, CS), F32),
            pltpu.VMEM((FAR, 16, CS), F32),
            pltpu.VMEM((FAR, 16, CS), F32),
        ],
    )(main, extra)


def gather_kernel(
    pos, seg, rad, cur, slot, pair, flag, main_all, extra_all, stack, send_sem, recv_sem
):
    row_count, col_count = lax.axis_size("row"), lax.axis_size("col")
    row, col = lax.axis_index("row"), lax.axis_index("col")
    me = row * col_count + col
    chips = row_count // 2
    other = row + 1 - 2 * lax.rem(row, 2)
    gathered = (main_all, extra_all)

    def row_at(base, step):
        return lax.rem(base + 2 * step, row_count)

    def col_at(step):
        return lax.rem(col + step, col_count)

    barrier = pltpu.get_barrier_semaphore()
    peers = [(row, col_at(k)) for k in range(1, col_count)]
    peers += [(row_at(row, k), col) for k in range(1, chips)] + [(other, col)]
    for to_row, to_col in peers:
        pl.semaphore_signal(
            barrier, inc=1, device_id={"row": to_row, "col": to_col}, device_id_type=MESH
        )
    order_into(
        pos, seg, rad, cur, slot, pair, flag, main_all.at[me], extra_all.at[me], stack
    )
    pl.semaphore_wait(barrier, len(peers))

    def copies(origin, lane, to_row, to_col):
        return [
            pltpu.make_async_remote_copy(
                src_ref=target.at[origin],
                dst_ref=target.at[origin],
                send_sem=send_sem.at[part, lane],
                recv_sem=recv_sem.at[part, origin],
                device_id={"row": to_row, "col": to_col},
                device_id_type=MESH,
            )
            for part, target in enumerate(gathered)
        ]

    sent = []

    def push(origin, to_row, to_col):
        started = copies(origin, len(sent), to_row, to_col)
        for copy in started:
            copy.start()
        sent.append(started)

    def arrive(origin):
        for copy in copies(origin, 0, other, col):
            copy.wait_recv()

    def fan_out(origin):
        for k in range(1, chips):
            push(origin, row_at(row, k), col)
        push(origin, other, col)

    for k in range(1, col_count):
        push(me, row, col_at(k))
    fan_out(me)
    for k in range(1, col_count):
        origin = row * col_count + col_at(col_count - k)
        arrive(origin)
        fan_out(origin)
    for block in range(col_count):
        for k in range(1, chips):
            origin = row_at(row, chips - k) * col_count + col_at(col_count - block)
            arrive(origin)
            push(origin, other, col)
    for block in range(col_count):
        for k in range(chips):
            arrive(row_at(other, chips - k) * col_count + col_at(col_count - block))
    for started in sent:
        for copy in started:
            copy.wait_send()


def gather_all(positions, segments, radius, currents, slot_of, pair_list, near_flag):
    row_count, col_count = lax.axis_size("row"), lax.axis_size("col")
    devices = row_count * col_count
    local = positions.shape[1]
    clusters = local // CS
    lanes = col_count - 1 + col_count * (row_count - 1)
    return pl.pallas_call(
        gather_kernel,
        out_shape=(
            jax.ShapeDtypeStruct((devices, clusters, 8, CS), F32),
            jax.ShapeDtypeStruct((devices, clusters + 2, CS), F32),
        ),
        in_specs=[VMEM] * 7,
        out_specs=(VMEM, VMEM),
        scratch_shapes=[
            pltpu.VMEM((48, local), F32),
            pltpu.SemaphoreType.DMA((2, lanes)),
            pltpu.SemaphoreType.DMA((2, devices)),
        ],
        compiler_params=pltpu.CompilerParams(collective_id=0, has_side_effects=True),
    )(
        positions,
        segments,
        radius[None, :],
        currents,
        slot_of[None, :],
        pair_list.T,
        near_flag[None, :],
    )


def scatter_kernel(
    total, resist, cur, slot, out, owned, arrived, chosen, stack, send_sem, recv_sem
):
    row_count, col_count = lax.axis_size("row"), lax.axis_size("col")
    devices = row_count * col_count
    clusters = owned.shape[0]
    me = lax.axis_index("row") * col_count + lax.axis_index("col")
    barrier = pltpu.get_barrier_semaphore()

    def call_on(step, _):
        peer = lax.rem(me + step, devices)
        pl.semaphore_signal(
            barrier,
            inc=1,
            device_id={"row": peer // col_count, "col": lax.rem(peer, col_count)},
            device_id_type=MESH,
        )
        return 0

    lax.fori_loop(1, devices, call_on, 0)
    slots = slot[...]
    for cluster in range(clusters):
        chosen[cluster] = one_hot_rows(slots, cluster * CS, CS)
    stack[...] = jnp.zeros_like(stack)
    pl.semaphore_wait(barrier, devices - 1)

    def copy_of(step):
        peer = lax.rem(me + step, devices)
        return pltpu.make_async_remote_copy(
            src_ref=total.at[pl.ds(peer * clusters, clusters)],
            dst_ref=arrived.at[step],
            send_sem=send_sem.at[step],
            recv_sem=recv_sem.at[step],
            device_id={"row": peer // col_count, "col": lax.rem(peer, col_count)},
            device_id_type=MESH,
        )

    def begin(step, _):
        copy_of(step).start()
        return 0

    lax.fori_loop(1, devices, begin, 0)
    owned[...] = total[pl.ds(me * clusters, clusters)]

    def collect(step, _):
        copy_of(step).wait_recv()
        owned[...] += arrived[step]
        return 0

    lax.fori_loop(1, devices, collect, 0)
    sums = jnp.zeros((16, slots.shape[1]), F32)
    for cluster in range(clusters):
        for part, piece in enumerate(split_three(owned[cluster])):
            stack[2 * part : 2 * part + 2, :] = piece
        sums = sums + dot_nn(stack[...].astype(BF16), chosen[cluster])
    induced = sums[0:2] + sums[2:4] + sums[4:6]
    scaled = resist[...] * cur[...]
    out[0:1, :] = scaled[0:1] - induced[1:2]
    out[1:2, :] = scaled[1:2] + induced[0:1]

    def end(step, _):
        copy_of(step).wait_send()
        return 0

    lax.fori_loop(1, devices, end, 0)


def scatter_finish(total, resist, currents, slot_of):
    devices = lax.axis_size("row") * lax.axis_size("col")
    local = currents.shape[1]
    clusters = local // CS
    return pl.pallas_call(
        scatter_kernel,
        out_shape=jax.ShapeDtypeStruct(currents.shape, F32),
        in_specs=[VMEM] * 4,
        out_specs=VMEM,
        scratch_shapes=[
            pltpu.VMEM((clusters,) + total.shape[1:], F32),
            pltpu.VMEM((devices, clusters) + total.shape[1:], F32),
            pltpu.VMEM((clusters, CS, local), BF16),
            pltpu.VMEM((16, CS), F32),
            pltpu.SemaphoreType.DMA((devices,)),
            pltpu.SemaphoreType.DMA((devices,)),
        ],
        compiler_params=pltpu.CompilerParams(collective_id=1, has_side_effects=True),
    )(total, resist[None, :], currents, slot_of[None, :])


def on_device(positions, segments, radius, currents, resist, slot_of, pair_list, near_flag):
    main_all, extra_all = gather_all(
        positions, segments, radius, currents, slot_of, pair_list, near_flag
    )
    total = pair_terms(main_all, extra_all)
    return scatter_finish(total, resist, currents, slot_of)


def solution(mesh):
    return jax.shard_map(
        on_device,
        mesh=mesh,
        in_specs=(
            P(None, ("row", "col")),
            P(None, ("row", "col")),
            P(("row", "col")),
            P(None, ("row", "col")),
            P(("row", "col")),
            P(("row", "col")),
            P(("row", "col"), None),
            P(("row", "col")),
        ),
        out_specs=P(None, ("row", "col")),
        check_vma=False,
    )
```

profile of v0, /device:TPU:0, one launch (start us, length us, event | category | flops | bytes accessed | tf_op | source)
XLA Modules:
  0.0 52.5 jit_solution(119233215152020602)
XLA Ops:
  0.0 19.0 %shard_map.82 = (f32[32,2,8,512]{3,2,1,0:T(8,128)}, f32[32,4,512]{2,1,0:T(4,128)}) custom-call(f32[3,1024]{1,0:T(4,128)} %pos.1, f32[3,1024]{1,0:T(4,128)} %seg.1, f32[1,1024]{1,0:T(1,128)} %bitcast.8, f32[2,1024]{1,0:T(2,128)} %cur.3, s32[1,1024]{1,0:T(1,128)} %bitcast.5, s32[2,32]{1,0:T(2,128)} %bitcast.9, s32[1,32]{1,0:T(1,128)} %bitcast.10), custom_call_target="tpu_custom_call" | custom-call | tf_op jit(solution)/shard_map/pallas_call | solution.py:323
  19.0 19.5 %shard_map.83.total = f32[64,2,512]{2,1,0:T(2,128)} custom-call(f32[32,2,8,512]{3,2,1,0:T(8,128)} %get-tuple-element.7.main, f32[32,4,512]{2,1,0:T(4,128)} %get-tuple-element.8.extra), custom_call_target="tpu_custom_call" | custom-call | tf_op jit(solution)/shard_map/pallas_call | solution.py:225
  38.4 12.8 %shard_map.84 = f32[2,1024]{1,0:T(2,128)} custom-call(f32[64,2,512]{2,1,0:T(2,128)} %shard_map.83.total, f32[1,1024]{1,0:T(1,128)} %bitcast.7, f32[2,1024]{1,0:T(2,128)} %cur.3, s32[1,1024]{1,0:T(1,128)} %bitcast.6), custom_call_target="tpu_custom_call" | custom-call | tf_op jit(solution)/shard_map/pallas_call | solution.py:419
  51.2 1.3 %copy.10 = f32[2,1024]{1,0:T(2,128)} copy(f32[2,1024]{1,0:T(2,128)} %shard_map.84) | data formatting | bytes 16384
where the time goes:
time: 52.8 us; the launch traced here: 52.5 us
  Pallas kernels  51.2 us (97%)
  local copies, waits for them, and re-layouts  1.3 us (2%)
    pallas_call x1, Pallas kernels, pair_terms(): pl.pallas_call(pair_kernel, out_shape=jax.ShapeDtypeStruct((devices * clu...  19.5 us
    pallas_call x1, Pallas kernels, gather_all(): pl.pallas_call(gather_kernel, out_shape=(jax.ShapeDtypeStruct((devices, c...  19 us
    pallas_call x1, Pallas kernels, scatter_finish(): pl.pallas_call(scatter_kernel, out_shape=jax.ShapeDtypeStruct(currents.sh...  12.8 us
    unnamed x1, local copies, waits for them, and re-layouts  1.3 us

commit v1 on v0

v1 whole, which is shorter than its diff:
```python
import functools
import math

import jax
import jax.numpy as jnp
from jax import lax
from jax.experimental import pallas as pl
from jax.experimental.pallas import tpu as pltpu
from jax.sharding import PartitionSpec as P

CS = 512
F32 = jnp.float32
BF16 = jnp.bfloat16
MESH = pl.DeviceIdType.MESH
gauss_step = 0.5 / math.sqrt(3.0)
kernel_gain = 0.25
VMEM = pl.BlockSpec(memory_space=pltpu.VMEM)
TALL = 256
STEP = 128
FAR = 2


def split_three(value):
    high = value.astype(BF16).astype(F32)
    rest = value - high
    middle = rest.astype(BF16).astype(F32)
    return high, middle, rest - middle


def dot_nn(left, right):
    return lax.dot_general(left, right, (((1,), (0,)), ((), ())), preferred_element_type=F32)


def dot_nt(left, right):
    return lax.dot_general(left, right, (((1,), (1,)), ((), ())), preferred_element_type=F32)


def one_hot_rows(slots, start, count):
    rows = lax.broadcasted_iota(jnp.int32, (count, slots.shape[1]), 0) + start
    return jnp.where(rows == slots, 1.0, 0.0).astype(BF16)


def order_into(pos, seg, rad, cur, slot, pair, flag, main, extra, stack):
    clusters = main.shape[0]
    slots = slot[...]
    stack[...] = jnp.zeros_like(stack)
    for source, row in ((pos, 0), (seg, 3), (rad, 6), (cur, 7)):
        count = source.shape[0]
        for part, piece in enumerate(split_three(source[...])):
            stack[part * 16 + row : part * 16 + row + count, :] = piece
    parts = stack[...].astype(BF16)
    for cluster in range(clusters):
        sums = dot_nt(parts, one_hot_rows(slots, cluster * CS, CS))
        ordered = sums[0:16] + sums[16:32] + sums[32:48]
        main[cluster] = ordered[0:8]
        extra[cluster : cluster + 1, :] = ordered[8:9]
    listed = pair.shape[1]
    extra[clusters : clusters + 2, :] = jnp.zeros((2, CS), F32)
    extra[clusters : clusters + 1, 0:listed] = pair[0:1, :].astype(F32)
    extra[clusters : clusters + 1, 128 : 128 + listed] = pair[1:2, :].astype(F32)
    extra[clusters : clusters + 1, 256 : 256 + listed] = flag[...].astype(F32)


def tile_rows(count):
    return lax.broadcasted_iota(jnp.int32, (8, count), 0)


def pair_kernel(
    main, extra, resist, cur, slot, out,
    acc, left, right, weight, retired, inverse, stack,
):
    devices, clusters = main.shape[0], main.shape[1]
    local = cur.shape[1]
    me = lax.axis_index("row") * lax.axis_size("col") + lax.axis_index("col")
    acc[...] = jnp.zeros_like(acc)
    retired[...] = jnp.zeros_like(retired)
    inverse[...] = jnp.zeros_like(inverse)
    rows = tile_rows(CS)

    lists = extra[:, clusters, :]
    first_ids, second_ids, flags = lists[:, 0:128], lists[:, 128:256], lists[:, 256:384]
    near_masks, far_masks, codes = [], [], []
    for k in range(clusters):
        own = (me * clusters + k).astype(F32)
        is_first = first_ids == own
        match = jnp.where(is_first | (second_ids == own), flags, 0.0)
        near_masks.append(jnp.where(match > 1.5, 1.0, 0.0))
        far_masks.append(jnp.where((match > 0.5) & (match < 1.5), 1.0, 0.0))
        codes.append(jnp.where(is_first, second_ids, first_ids) + 4096.0 * k)
    masks = jnp.concatenate(near_masks + far_masks, 0)
    code = jnp.concatenate(codes + codes, 0)
    marks = masks.astype(BF16)
    entries = masks.shape[0]
    before_lane = jnp.where(
        lax.broadcasted_iota(jnp.int32, (128, 128), 0) < lax.broadcasted_iota(jnp.int32, (128, 128), 1),
        1.0,
        0.0,
    ).astype(BF16)
    before_row = jnp.where(
        lax.broadcasted_iota(jnp.int32, (entries, entries), 1)
        < lax.broadcasted_iota(jnp.int32, (entries, entries), 0),
        1.0,
        0.0,
    ).astype(BF16)
    in_row = dot_nn(marks, jnp.ones((128, 128), BF16)).astype(BF16)
    rank = jnp.where(
        masks > 0.5, dot_nn(marks, before_lane) + dot_nn(before_row, in_row), -1.0
    ).astype(jnp.int32)
    near_count = jnp.sum(masks[0 : clusters * devices]).astype(jnp.int32)
    count = jnp.sum(masks).astype(jnp.int32)

    def pick(turn):
        return jnp.sum(jnp.where(rank == turn, code, 0.0)).astype(jnp.int32)

    def moved(block, turned, sign):
        points = block - 0.5
        if sign:
            points = points + (sign * gauss_step) * turned
        squares = jnp.where(rows < 3, points * points, jnp.where(rows == 3, turned * turned, 0.0))
        return points, jnp.sum(squares, axis=0, keepdims=True)

    def stacked(value, order):
        parts = split_three(value)
        return [
            jnp.concatenate([parts[order[n]], parts[order[n + 1]]], 0) for n in range(0, 6, 2)
        ]

    def left_side(block, turned, sign):
        points, norm = moved(block, turned, sign)
        value = jnp.where(rows < 3, points, jnp.where(rows == 3, norm, jnp.where(rows == 4, 1.0, 0.0)))
        return jnp.concatenate(stacked(value, (0, 0, 1, 1, 0, 2)), 0)

    def right_side(block, turned, sign):
        points, norm = moved(block, turned, sign)
        value = jnp.where(
            rows < 3, -2.0 * points, jnp.where(rows == 3, 1.0, jnp.where(rows == 4, norm, 0.0))
        )
        return stacked(value, (0, 1, 0, 1, 2, 0))

    def prepare(unit, now, scale, signs):
        cluster = now % 4096
        device, place = cluster // clusters, cluster % clusters
        block = main[device, place]
        imag = extra[device, pl.ds(place, 1), :]
        turned = pltpu.roll(block, 5, 0)
        for index, sign in enumerate(signs):
            for part, piece in enumerate(right_side(block, turned, sign)):
                right[unit, index, 16 * part : 16 * part + 16, :] = piece.astype(BF16)
        value = jnp.where(rows < 3, turned * block[7:8], jnp.where(rows < 6, block * imag, 0.0))
        value = value * scale
        high = value.astype(BF16).astype(F32)
        weight[unit] = jnp.concatenate([high, value - high], 0).astype(BF16)

    def retire(unit, k):
        weights = retired[unit]
        weights = jnp.concatenate([weights, weights], 1)
        for start in range(0, CS, TALL):
            term = dot_nt(weights, inverse[unit, start : start + TALL, :])
            acc[k, :, start : start + TALL] += term

    def compute(unit, k, lefts, count_right):
        sides = [right[unit, index] for index in range(count_right)]
        for start in range(0, CS, STEP):
            total = 0.0
            for variant in lefts:
                one = left[k, variant, start : start + STEP, :]
                for other in sides:
                    total = total + lax.rsqrt(dot_nn(one, other))
            high = total.astype(BF16)
            inverse[unit, start : start + STEP, 0:CS] = high
            inverse[unit, start : start + STEP, CS:] = (total - high.astype(F32)).astype(BF16)
        retired[unit] = weight[unit]

    for k in range(clusters):
        block = main[me, k]
        turned = pltpu.roll(block, 5, 0)
        for variant, sign in enumerate((0, -1, 1)):
            left[k, variant] = left_side(block, turned, sign).T.astype(BF16)

    near_gain, far_gain = kernel_gain * 0.25, kernel_gain

    def visit_near(turn, state):
        now, later, last = state
        retire(0, last)
        k = now // 4096
        compute(0, k, (1, 2), 2)
        prepare(0, later, near_gain, (-1, 1))
        return later, pick(turn + 2), k

    def far_scale(turn):
        return jnp.where(turn < count, far_gain, 0.0)

    def visit_far(step, state):
        turn = near_count + FAR * step
        nows, laters, lasts = state
        for unit in range(FAR):
            retire(unit, lasts[unit])
        ks = tuple(nows[unit] // 4096 for unit in range(FAR))
        for unit in range(FAR):
            compute(unit, ks[unit], (0,), 1)
        for unit in range(FAR):
            prepare(unit, laters[unit], far_scale(turn + FAR + unit), (0,))
        return laters, tuple(pick(turn + 2 * FAR + unit) for unit in range(FAR)), ks

    begin = pick(0)
    prepare(0, begin, near_gain, (-1, 1))
    _, _, last = lax.fori_loop(0, near_count, visit_near, (begin, pick(1), 0))
    nows = tuple(pick(near_count + unit) for unit in range(FAR))
    laters = tuple(pick(near_count + FAR + unit) for unit in range(FAR))
    for unit in range(FAR):
        prepare(unit, nows[unit], far_scale(near_count + unit), (0,))
    _, _, lasts = lax.fori_loop(
        0,
        (count - near_count + FAR - 1) // FAR,
        visit_far,
        (nows, laters, (last,) + (0,) * (FAR - 1)),
    )
    for unit in range(FAR):
        retire(unit, lasts[unit])

    tiles = CS // 128
    for k in range(clusters):
        both = acc[k, 0:8, :] + acc[k, 8:16, :]
        block = main[me, k]
        turned = pltpu.roll(block, 5, 0)
        real = jnp.sum(jnp.where(rows < 3, both * turned, 0.0), axis=0, keepdims=True)
        imag = jnp.sum(
            jnp.where((rows > 2) & (rows < 6), both * block, 0.0), axis=0, keepdims=True
        )
        for row, value in enumerate((real, imag)):
            for part, piece in enumerate(split_three(value)):
                for tile in range(tiles):
                    base = (part * 2 + row) * clusters * tiles + k * tiles + tile
                    stack[base : base + 1, :] = piece[:, 128 * tile : 128 * tile + 128]
    slots = slot[...]
    lanes = lax.rem(slots, 128)
    chosen = jnp.where(
        lax.broadcasted_iota(jnp.int32, (128, local), 0) == lanes, 1.0, 0.0
    ).astype(BF16)
    spread = dot_nn(stack[...].astype(BF16), chosen)
    height = clusters * tiles
    mine = lax.broadcasted_iota(jnp.int32, (height, local), 0) == slots // 128
    induced = []
    for row in range(2):
        whole = 0.0
        for part in range(3):
            base = (part * 2 + row) * height
            whole = whole + spread[base : base + height]
        induced.append(jnp.sum(jnp.where(mine, whole, 0.0), axis=0, keepdims=True))
    scaled = resist[...] * cur[...]
    out[0:1, :] = scaled[0:1] - induced[1]
    out[1:2, :] = scaled[1:2] + induced[0]


def pair_terms(main, extra, resist, currents, slot_of):
    clusters = main.shape[1]
    return pl.pallas_call(
        pair_kernel,
        out_shape=jax.ShapeDtypeStruct(currents.shape, F32),
        in_specs=[VMEM] * 5,
        out_specs=VMEM,
        scratch_shapes=[
            pltpu.VMEM((clusters, 16, CS), F32),
            pltpu.VMEM((clusters, 3, CS, 48), BF16),
            pltpu.VMEM((FAR, 2, 48, CS), BF16),
            pltpu.VMEM((FAR, 16, CS), BF16),
            pltpu.VMEM((FAR, 16, CS), BF16),
            pltpu.VMEM((FAR, CS, 2 * CS), BF16),
            pltpu.VMEM((6 * clusters * CS // 128, 128), F32),
        ],
    )(main, extra, resist[None, :], currents, slot_of[None, :])


def gather_kernel(
    pos, seg, rad, cur, slot, pair, flag, main_all, extra_all, stack, send_sem, recv_sem
):
    row_count, col_count = lax.axis_size("row"), lax.axis_size("col")
    row, col = lax.axis_index("row"), lax.axis_index("col")
    me = row * col_count + col
    chips = row_count // 2
    other = row + 1 - 2 * lax.rem(row, 2)
    gathered = (main_all, extra_all)

    def row_at(base, step):
        return lax.rem(base + 2 * step, row_count)

    def col_at(step):
        return lax.rem(col + step, col_count)

    barrier = pltpu.get_barrier_semaphore()
    peers = [(row, col_at(k)) for k in range(1, col_count)]
    peers += [(row_at(row, k), col) for k in range(1, chips)] + [(other, col)]
    for to_row, to_col in peers:
        pl.semaphore_signal(
            barrier, inc=1, device_id={"row": to_row, "col": to_col}, device_id_type=MESH
        )
    order_into(
        pos, seg, rad, cur, slot, pair, flag, main_all.at[me], extra_all.at[me], stack
    )
    pl.semaphore_wait(barrier, len(peers))

    def copies(origin, lane, to_row, to_col):
        return [
            pltpu.make_async_remote_copy(
                src_ref=target.at[origin],
                dst_ref=target.at[origin],
                send_sem=send_sem.at[part, lane],
                recv_sem=recv_sem.at[part, origin],
                device_id={"row": to_row, "col": to_col},
                device_id_type=MESH,
            )
            for part, target in enumerate(gathered)
        ]

    sent = []

    def push(origin, to_row, to_col):
        started = copies(origin, len(sent), to_row, to_col)
        for copy in started:
            copy.start()
        sent.append(started)

    def arrive(origin):
        for copy in copies(origin, 0, other, col):
            copy.wait_recv()

    def fan_out(origin):
        for k in range(1, chips):
            push(origin, row_at(row, k), col)
        push(origin, other, col)

    for k in range(1, col_count):
        push(me, row, col_at(k))
    fan_out(me)
    for k in range(1, col_count):
        origin = row * col_count + col_at(col_count - k)
        arrive(origin)
        fan_out(origin)
    for block in range(col_count):
        for k in range(1, chips):
            origin = row_at(row, chips - k) * col_count + col_at(col_count - block)
            arrive(origin)
            push(origin, other, col)
    for block in range(col_count):
        for k in range(chips):
            arrive(row_at(other, chips - k) * col_count + col_at(col_count - block))
    for started in sent:
        for copy in started:
            copy.wait_send()


def gather_all(positions, segments, radius, currents, slot_of, pair_list, near_flag):
    row_count, col_count = lax.axis_size("row"), lax.axis_size("col")
    devices = row_count * col_count
    local = positions.shape[1]
    clusters = local // CS
    lanes = col_count - 1 + col_count * (row_count - 1)
    return pl.pallas_call(
        gather_kernel,
        out_shape=(
            jax.ShapeDtypeStruct((devices, clusters, 8, CS), F32),
            jax.ShapeDtypeStruct((devices, clusters + 2, CS), F32),
        ),
        in_specs=[VMEM] * 7,
        out_specs=(VMEM, VMEM),
        scratch_shapes=[
            pltpu.VMEM((48, local), F32),
            pltpu.SemaphoreType.DMA((2, lanes)),
            pltpu.SemaphoreType.DMA((2, devices)),
        ],
        compiler_params=pltpu.CompilerParams(collective_id=0, has_side_effects=True),
    )(
        positions,
        segments,
        radius[None, :],
        currents,
        slot_of[None, :],
        pair_list.T,
        near_flag[None, :],
    )


def on_device(positions, segments, radius, currents, resist, slot_of, pair_list, near_flag):
    main_all, extra_all = gather_all(
        positions, segments, radius, currents, slot_of, pair_list, near_flag
    )
    return pair_terms(main_all, extra_all, resist, currents, slot_of)


def solution(mesh):
    return jax.shard_map(
        on_device,
        mesh=mesh,
        in_specs=(
            P(None, ("row", "col")),
            P(None, ("row", "col")),
            P(("row", "col")),
            P(None, ("row", "col")),
            P(("row", "col")),
            P(("row", "col")),
            P(("row", "col"), None),
            P(("row", "col")),
        ),
        out_specs=P(None, ("row", "col")),
        check_vma=False,
    )
```

time: 52.8 us -> 50.3 us (0.953)
  Pallas kernels: 51.2 us -> 49.8 us
  local copies, waits for them, and re-layouts: 1.3 us -> 0 us
    pallas_call x2 -> x1, Pallas kernels: 32.2 us -> 30.9 us  [pair_terms(): pl.pallas_call(pair_kernel, out_shape=jax.ShapeDtypeStruct(currents.shape...]
    unnamed x1 -> x0, local copies, waits for them, and re-layouts: 1.3 us -> none
where the time goes in v1:
time: 50.3 us; the launch traced here: 49.8 us
  Pallas kernels  49.8 us (99%)
    pallas_call x1, Pallas kernels, pair_terms(): pl.pallas_call(pair_kernel, out_shape=jax.ShapeDtypeStruct(currents.shape...  30.9 us
    pallas_call x1, Pallas kernels, gather_all(): pl.pallas_call(gather_kernel, out_shape=(jax.ShapeDtypeStruct((devices, c...  19 us

profile of v1, /device:TPU:0, one launch (start us, length us, event | category | flops | bytes accessed | tf_op | source)
XLA Modules:
  0.0 49.8 jit_solution(17976060381864605220)
XLA Ops:
  0.0 19.0 %shard_map.82 = (f32[32,2,8,512]{3,2,1,0:T(8,128)}, f32[32,4,512]{2,1,0:T(4,128)}) custom-call(f32[3,1024]{1,0:T(4,128)} %pos.1, f32[3,1024]{1,0:T(4,128)} %seg.1, f32[1,1024]{1,0:T(1,128)} %bitcast.8, f32[2,1024]{1,0:T(2,128)} %cur.3, s32[1,1024]{1,0:T(1,128)} %bitcast.5, s32[2,32]{1,0:T(2,128)} %bitcast.9, s32[1,32]{1,0:T(1,128)} %bitcast.10), custom_call_target="tpu_custom_call" | custom-call | tf_op jit(solution)/shard_map/pallas_call | solution.py:358
  19.0 30.9 %shard_map.83 = f32[2,1024]{1,0:T(2,128)} custom-call(f32[32,2,8,512]{3,2,1,0:T(8,128)} %get-tuple-element.7.main, f32[32,4,512]{2,1,0:T(4,128)} %get-tuple-element.8.extra, f32[1,1024]{1,0:T(1,128)} %bitcast.7, f32[2,1024]{1,0:T(2,128)} %cur.3, s32[1,1024]{1,0:T(1,128)} %bitcast.6), custom_call_target="tpu_custom_call" | custom-call | tf_op jit(solution)/shard_map/pallas_call | solution.py:257
